TPU v7x, 32 devices: a whole 2x2x4 slice. The times are simulated.
32 devices in a mesh: gx: 4 (over y, x), gy: 4 (over z), ga: 2 (over core).
Axes of the slice: x: 2, y: 2, z: 4, core: 2. Of those that a mesh axis runs over, the one named last changes fastest.
Arguments:
- fields: float32 [5, 16, 64, 1024], P(None, 'ga', 'gx', 'gy'), may hold values from -6 to 6
- stiffness: float32 [16, 64, 1024], P('ga', 'gx', 'gy'), may hold values from 0.25 to 4
- lift_weight: float32 [5, 32], replicated, may hold values from -2.5 to 2.5
- lift_bias: float32 [32], replicated, may hold values from -3 to 3
- mix_weight: bfloat16 [32, 32], replicated, may hold values from -0.5 to 0.5
- spectral_weight: float32 [8, 32, 32, 32, 128], P('ga', 'gy', None, 'gx'), may hold values from -0.48 to 0.48
- output_bias: float32 [32], replicated, may hold values from -3 to 3
Outputs:
- layer_out: bfloat16 [16, 32, 32, 512], P('ga', None, 'gx', 'gy')
All inputs are finite; a program needn't handle non-finite values.
Results may differ from a plain program's by a relative error of at most 0.01.
Values may be sent and summed in bfloat16 or wider, within the bound.
A program may use at most 128 MiB of HBM per device.

v0:
```python
import math
import jax
import jax.numpy as jnp
from jax import lax
from jax.sharding import PartitionSpec as P

STEPS = 3
MX = 32
MY = 64
MZ = 8
courant_half = 0.1
smooth_half = 0.15
mean_flow = (0.3, -0.2, 0.1)
highest = lax.Precision.HIGHEST


def padded_2(block, sides, width):
    for axis, dim in sides:
        count = lax.axis_size(axis)
        forward = [(i, i + 1) for i in range(count - 1)]
        forward.append((count - 1, 0))
        backward = [(target, source) for source, target in forward]
        low = lax.ppermute(
            lax.slice_in_dim(block, block.shape[dim] - width, None, axis=dim), axis, forward
        )
        high = lax.ppermute(lax.slice_in_dim(block, 0, width, axis=dim), axis, backward)
        block = jnp.concatenate([low, block, high], axis=dim)
    return block


def step_interior(padded, stiff_part):
    center = padded[:, 1:-1, 1:-1, 1:-1]
    upper_depth = padded[:, 2:, 1:-1, 1:-1]
    lower_depth = padded[:, :-2, 1:-1, 1:-1]
    upper_east = padded[:, 1:-1, 2:, 1:-1]
    lower_east = padded[:, 1:-1, :-2, 1:-1]
    upper_north = padded[:, 1:-1, 1:-1, 2:]
    lower_north = padded[:, 1:-1, 1:-1, :-2]
    slope_depth = upper_depth - lower_depth
    slope_east = upper_east - lower_east
    slope_north = upper_north - lower_north
    curvature = (
        upper_depth
        + lower_depth
        + upper_east
        + lower_east
        + upper_north
        + lower_north
        - 6.0 * center
    )
    transport = mean_flow[0] * slope_east + mean_flow[1] * slope_north + mean_flow[2] * slope_depth
    diverge = slope_east[1] + slope_north[2] + slope_depth[3]
    coupling = jnp.stack(
        [diverge, slope_east[4], slope_north[4], slope_depth[4], stiff_part * diverge]
    )
    return center - courant_half * (transport + coupling) + smooth_half * curvature


def trim(block, margin):
    return block[margin:-margin, margin:-margin, margin:-margin]


def coarsen(fields_now):
    extent = fields_now.shape
    blocks = fields_now.reshape(extent[0], extent[1], extent[2] // 2, 2, extent[3] // 2, 2)
    return 0.25 * (
        blocks[:, :, :, 0, :, 0]
        + blocks[:, :, :, 1, :, 0]
        + blocks[:, :, :, 0, :, 1]
        + blocks[:, :, :, 1, :, 1]
    )


def angles(frequencies, points, length):
    product = jnp.mod(frequencies[:, None] * points[None, :], length)
    return product.astype(jnp.float32) * (2.0 * math.pi / length)


def centered(number):
    return jnp.arange(number, dtype=jnp.int32) - number // 2


def forward_east_table(points, length, mode_count):
    phases = angles(centered(mode_count), points, length)
    factor = 1.0 / math.sqrt(length)
    return (jnp.stack([jnp.cos(phases).T, -jnp.sin(phases).T], axis=1) * factor).astype(
        jnp.bfloat16
    )


def forward_north_table(points, length, mode_count):
    phases = angles(centered(mode_count), points, length)
    factor = 1.0 / math.sqrt(length)
    cosines = jnp.cos(phases).T * factor
    sines = jnp.sin(phases).T * factor
    return jnp.stack(
        [jnp.concatenate([cosines, -sines], axis=1), jnp.concatenate([sines, cosines], axis=1)],
        axis=0,
    )


def inverse_north_table(points, length, mode_count):
    phases = angles(centered(mode_count), points, length)
    factor = 1.0 / math.sqrt(length)
    cosines = jnp.cos(phases) * factor
    sines = jnp.sin(phases) * factor
    return jnp.concatenate(
        [jnp.stack([cosines, sines], axis=1), jnp.stack([-sines, cosines], axis=1)], axis=0
    )


def inverse_east_table(points, length, mode_count):
    phases = angles(centered(mode_count), points, length)
    factor = 1.0 / math.sqrt(length)
    return jnp.stack([jnp.cos(phases) * factor, -jnp.sin(phases) * factor], axis=1)


def forward_depth_blocks(values, points, frequencies, length):
    slot_count = frequencies.shape[0]
    phases = angles(frequencies.reshape(-1), points, length).reshape(
        slot_count, frequencies.shape[1], points.shape[0]
    )
    factor = 1.0 / math.sqrt(length)
    cosines = jnp.cos(phases) * factor
    sines = jnp.sin(phases) * factor
    halfway = values.shape[-1] // 2
    real_in = values[..., :halfway]
    imag_in = values[..., halfway:]
    real_part = jnp.einsum("zcrbn,rkz->rkcbn", real_in, cosines, precision=highest) + jnp.einsum(
        "zcrbn,rkz->rkcbn", imag_in, sines, precision=highest
    )
    imag_part = jnp.einsum("zcrbn,rkz->rkcbn", imag_in, cosines, precision=highest) - jnp.einsum(
        "zcrbn,rkz->rkcbn", real_in, sines, precision=highest
    )
    return jnp.concatenate([real_part, imag_part], axis=-1)


def mix_channels(coeffs, weight):
    halfway = coeffs.shape[-1] // 2
    real_in = coeffs[..., :halfway]
    imag_in = coeffs[..., halfway:]
    weight_real = weight[..., :halfway]
    weight_imag = weight[..., halfway:]
    real_part = jnp.einsum(
        "kcmn,kmcon->komn", real_in, weight_real, precision=highest
    ) - jnp.einsum("kcmn,kmcon->komn", imag_in, weight_imag, precision=highest)
    imag_part = jnp.einsum(
        "kcmn,kmcon->komn", imag_in, weight_real, precision=highest
    ) + jnp.einsum("kcmn,kmcon->komn", real_in, weight_imag, precision=highest)
    return jnp.concatenate([real_part, imag_part], axis=-1)


def inverse_depth(values, frequencies, points, length):
    phases = angles(frequencies, points, length)
    factor = 1.0 / math.sqrt(length)
    cosines = jnp.cos(phases) * factor
    sines = jnp.sin(phases) * factor
    halfway = values.shape[-1] // 2
    real_in = values[..., :halfway]
    imag_in = values[..., halfway:]
    real_part = jnp.einsum("komn,kz->zomn", real_in, cosines, precision=highest) - jnp.einsum(
        "komn,kz->zomn", imag_in, sines, precision=highest
    )
    imag_part = jnp.einsum("komn,kz->zomn", imag_in, cosines, precision=highest) + jnp.einsum(
        "komn,kz->zomn", real_in, sines, precision=highest
    )
    return jnp.concatenate([real_part, imag_part], axis=-1)


def shards(fields, stiffness, lift_weight, lift_bias, mix_weight, spectral_weight, output_bias):
    east_tiles = lax.axis_size("gx")
    north_tiles = lax.axis_size("gy")
    depth_groups = lax.axis_size("ga")
    stacked = jnp.concatenate([fields, stiffness[None]], axis=0)
    padded = padded_2(stacked, (("gx", 2), ("gy", 3), ("ga", 1)), STEPS)
    fields_now = padded[:5]
    for repeat in range(STEPS):
        fields_now = step_interior(fields_now, trim(padded[5], repeat + 1))
    filtered = coarsen(fields_now)
    pre_lift = (
        jnp.einsum("fzxy,fc->zcxy", filtered, lift_weight, precision=highest)
        + lift_bias[None, :, None, None]
    )
    lifted = jax.nn.gelu(pre_lift, approximate=True).astype(jnp.bfloat16)
    depth_local = lifted.shape[0]
    length_east = lifted.shape[2] * east_tiles
    length_north = lifted.shape[3] * north_tiles
    length_depth = depth_local * depth_groups
    east_points = jnp.arange(length_east, dtype=jnp.int32)
    north_points = jnp.arange(length_north, dtype=jnp.int32)
    table_east = forward_east_table(east_points, length_east, MX)
    table_north = forward_north_table(north_points, length_north, MY)
    planes = lax.all_to_all(
        lax.all_to_all(lifted, "gx", split_axis=1, concat_axis=2, tiled=True),
        "gy",
        split_axis=0,
        concat_axis=3,
        tiled=True,
    )
    east_modes = jnp.einsum(
        "zcxy,xpm->zcpmy", planes, table_east, preferred_element_type=jnp.float32
    )
    north_modes = jnp.einsum("zcpmy,pyq->zcmq", east_modes, table_north, precision=highest)
    plane_count = planes.shape[0]
    depth_points = (
        lax.axis_index("ga") * depth_local
        + lax.axis_index("gy") * plane_count
        + jnp.arange(plane_count, dtype=jnp.int32)
    )
    block_east = MX // north_tiles
    block_depth = MZ // depth_groups
    grouped = north_modes.reshape(
        plane_count, north_modes.shape[1], north_tiles, block_east, 2 * MY
    )
    owners = jnp.arange(1 * lax.axis_size(("gy", "ga")), dtype=jnp.int32)
    picked = jnp.take(grouped, owners // depth_groups, axis=2)
    frequencies = (owners % depth_groups)[:, None] * block_depth + jnp.arange(
        block_depth, dtype=jnp.int32
    )[None, :]
    coeffs = lax.psum_scatter(
        forward_depth_blocks(picked, depth_points, frequencies, length_depth).astype(jnp.bfloat16),
        ("gy", "ga"),
        scatter_dimension=0,
        tiled=True,
    ).astype(jnp.float32)[0]
    mixed_modes = mix_channels(lax.all_gather(coeffs, "gx", axis=1, tiled=True), spectral_weight)
    own_frequencies = lax.axis_index("ga") * coeffs.shape[0] + jnp.arange(
        coeffs.shape[0], dtype=jnp.int32
    )
    points = jnp.arange(depth_local * lax.axis_size("ga"), dtype=jnp.int32)
    back_depth = lax.psum_scatter(
        inverse_depth(mixed_modes, own_frequencies, points, length_depth),
        "ga",
        scatter_dimension=0,
        tiled=True,
    )
    back_north = jnp.einsum(
        "zomq,qpy->zompy",
        back_depth,
        inverse_north_table(north_points, length_north, MY),
        precision=highest,
    )
    all_modes = lax.all_to_all(back_north, "gy", split_axis=4, concat_axis=2, tiled=True)
    spectral = jnp.einsum(
        "zompy,mpx->zoxy",
        all_modes,
        inverse_east_table(east_points, length_east, MX),
        precision=highest,
    ).astype(jnp.bfloat16)
    spectral = lax.all_to_all(spectral, "gx", split_axis=2, concat_axis=1, tiled=True)
    direct = jnp.einsum("zcxy,co->zoxy", lifted, mix_weight, preferred_element_type=jnp.float32)
    summed = direct + output_bias[None, :, None, None] + spectral.astype(jnp.float32)
    return jax.nn.gelu(summed, approximate=True).astype(jnp.bfloat16)


def solution(mesh):
    placed = (
        P(None, "ga", "gx", "gy"),
        P("ga", "gx", "gy"),
        P(),
        P(),
        P(),
        P("ga", "gy", None, "gx", None),
        P(),
    )
    return jax.shard_map(
        shards, mesh=mesh, in_specs=placed, out_specs=P("ga", None, "gx", "gy"), check_vma=False
    )
```

profile of v0, /device:TPU:0, one launch (start us, length us, event | category | flops | bytes accessed | tf_op | source)
XLA Modules:
  0.0 479.2 jit_solution(17202555115786274294)
XLA Ops:
  6.5 1.2 fusion.67
  7.8 3.0 collective-permute-start
  10.9 1.0 collective-permute-start.1
  11.9 1.0 pad_maximum_fusion.2
  12.9 4.0 copy.86
  16.8 4.0 copy.85
  20.8 4.0 copy.87
  24.8 1.4 pad_maximum_fusion.7
  26.2 2.1 collective-permute-start.2
  28.3 2.3 collective-permute-start.3
  30.5 2.7 collective-permute-done.2
  33.5 6.5 %pad_maximum_fusion = f32[6,8,22,262]{2,1,3,0:T(8,128)S(1)} fusion(f32[6,8,22,3]{2,1,3,0:T(8,128)S(1)} %collective-permute-done.3, f32[6,8,3,256]{2,1,3,0:T(8,128)S(1)} %copy-done.2, f32[6,8,16,256]{2,1,3,0:T(8,128)} %copy.86, f32[6,8,3,256]{2,1,3,0:T(8,128)} %copy.85, f32[6,8,22,3]{2,1,3,0:T(8,128)S(1)} %collective-permute-done.2), kind=kLoop, calls=%fused_computation.1 | loop fusion | flops 1106688 | bytes 2213376 | tf_op jit(solution)/shard_map/concatenate | solution.py:27
  40.0 3.1 fusion.167
  43.8 4.0 copy.88
  47.8 2.3 copy.89
  50.6 5.1 %copy.90 = f32[6,8,22,262]{3,2,1,0:T(8,128)S(1)} copy(f32[6,8,22,262]{2,1,3,0:T(8,128)} %copy-done.1) | data formatting | bytes 2213376 | tf_op jit(solution)/shard_map/concatenate | solution.py:27
  55.7 1.3 pad_maximum_fusion.1
  57.0 3.0 slice_subtract_fusion.2
  60.5 4.1 multiply_add_fusion
  64.6 2.5 slice_subtract_fusion.5
  67.5 3.3 multiply_add_fusion.1
  70.8 0.9 slice_subtract_fusion.8
  71.9 1.2 multiply_add_fusion.2
  73.1 5.5 %copy.91 = f32[5,8,16,256]{1,3,2,0:T(8,128)} copy(f32[5,8,16,256]{3,2,1,0:T(8,128)S(1)} %multiply_add_fusion.2) | data formatting | bytes 1310720 | tf_op jit(solution)/shard_map/add | solution.py:56
  78.6 10.9 %fusion = f32[5,8,8,1,128,1]{1,5,4,3,2,0:T(1,128)S(1)} fusion(f32[5,8,8,2,128,2]{1,5,4,3,2,0:T(2,128)} %bitcast.187), kind=kLoop, calls=%fused_computation.8 | loop fusion | flops 163840 | bytes 819200 | tf_op jit(solution)/shard_map/mul | solution.py:66
  89.5 1.1 copy.92
  90.7 1.3 fusion.29
  92.0 1.0 copy.94
  93.0 3.5 all-to-all-start
  96.5 8.4 %all-to-all-done = bf16[8,32,8,128]{3,2,0,1:T(8,128)(2,1)S(1)} async-done(((bf16[8,32,8,128]{3,2,0,1:T(8,128)(2,1)}), bf16[8,32,8,128]{3,2,0,1:T(8,128)(2,1)S(1)}, u32[]{:S(2)}, u32[]{:S(2)}) %all-to-all-start) | async-done | bytes 524320 | tf_op jit(solution)/shard_map/all_to_all | solution.py:194
  104.9 0.9 copy.199
  105.8 4.4 all-to-all-start.1
  110.7 1.1 fusion.83
  112.2 11.9 %all-to-all-done.1 = bf16[8,8,32,128]{3,2,1,0:T(8,128)(2,1)S(1)} async-done(((bf16[8,8,32,128]{3,2,1,0:T(8,128)(2,1)}), bf16[8,8,32,128]{3,2,1,0:T(8,128)(2,1)S(1)}, u32[]{:S(2)}, u32[]{:S(2)}) %all-to-all-start.1) | async-done | bytes 524320 | tf_op jit(solution)/shard_map/all_to_all | solution.py:193
  125.2 1.8 fusion.19
  127.0 0.6 gather_fusion
  128.3 2.4 fusion.56
  130.6 3.0 fusion.52
  133.6 3.3 fusion.14
  136.9 2.5 fusion.15
  139.4 0.7 pad_maximum_fusion.3
  140.2 0.9 copy.99
  141.2 29.5 %reduce-scatter.3.cloned.1.call-done = bf16[1,4,8,8,128]{4,3,2,1,0:T(8,128)(2,1)} async-done(((bf16[8,4,8,8,128]{4,3,2,1,0:T(8,128)(2,1)}), bf16[1,4,8,8,128]{4,3,2,1,0:T(8,128)(2,1)}) %reduce-scatter.3.cloned.1.call-update) | async-done | bytes 65552 | tf_op jit(solution)/shard_map/reduce_scatter | solution.py:220
  170.7 0.8 copy.100
  171.5 10.2 %all-gather = f32[1,4,32,8,128]{4,3,1,0,2:T(8,128)S(1)} all-gather(f32[1,4,8,8,128]{4,3,1,0,2:T(8,128)S(1)} %copy.100), channel_id=2, replica_groups=mesh['gx'=4,'gy'=4,'ga'=2] {'gx'}, dimensions={2}, use_global_device_ids=true | all-gather | bytes 655360 | tf_op jit(solution)/shard_map/all_gather | solution.py:226
  182.5 1.3 copy-done.3
  183.9 2.4 multiply_reduce_fusion.3
  186.3 0.9 fusion.78
  187.2 0.9 fusion.74
  188.1 0.9 convolution_subtract_fusion.1
  189.0 0.9 convolution_add_fusion.3
  189.8 1.0 pad_maximum_fusion.4
  191.5 5.3 %reduce-scatter.5.cloned.1.call-done = f32[8,8,8,128]{3,0,2,1:T(8,128)} async-done(((f32[16,8,8,128]{3,0,2,1:T(8,128)}), f32[8,8,8,128]{3,0,2,1:T(8,128)}) %reduce-scatter.5.cloned.1.call-update) | async-done | bytes 262160 | tf_op jit(solution)/shard_map/reduce_scatter | solution.py:231
  196.8 2.7 fusion.40
  199.5 23.9 %copy.102 = f32[8,8,8,2,512]{2,3,1,0,4:T(2,128)} copy(f32[8,8,8,2,512]{4,0,3,2,1:T(8,128)S(1)} %fusion.40) | data formatting | bytes 4194304 | tf_op jit(solution)/shard_map/zomq,qpy->zompy/dot_general | solution.py:237
  223.4 66.8 %reshape.480 = f32[4,1,131072]{2,1,0:T(1,128)S(1)} reshape(f32[512,8,8,2,8]{4,3,2,1,0:T(2,128)} %bitcast.185) | data formatting | bytes 4194304
  290.3 53.4 %all_to_all.63 = f32[4,1,131072]{2,1,0:T(1,128)} all-to-all(f32[4,1,131072]{2,1,0:T(1,128)S(1)} %reshape.480), channel_id=1, replica_groups=mesh['gx'=4,'gy'=4,'ga'=2] {'gy'}, dimensions={0} | all-to-all | bytes 4194304 | tf_op jit(solution)/shard_map/all_to_all | solution.py:243
  344.2 7.7 %reduce.8 = f32[4,131072]{1,0:T(4,128)S(1)} reduce(f32[4,1,131072]{2,1,0:T(1,128)} %all_to_all.63, f32[]{:T(128)} %broadcast.796), dimensions={1}, to_apply=%all_to_all.54.reduce_sub_computation | reduce | bytes 4194308 | tf_op jit(solution)/shard_map/all_to_all | solution.py:243
  351.9 65.7 %reshape.481 = f32[512,8,8,2,8]{4,3,2,1,0:T(2,128)} reshape(f32[4,131072]{1,0:T(4,128)S(1)} %reduce.8) | data formatting | bytes 4194304
  417.6 40.1 %copy.103 = f32[8,8,8,2,4,128]{5,2,4,3,1,0:T(8,128)S(1)} copy(f32[8,8,8,2,4,128]{2,3,1,0,5,4:T(2,128)} %bitcast.186) | data formatting | bytes 4194304 | tf_op jit(solution)/shard_map/all_to_all | solution.py:243
  457.7 1.1 fusion.16
  459.1 11.4 %all_to_all.64 = bf16[8,8,32,128]{3,1,0,2:T(8,128)(2,1)S(1)} all-to-all(bf16[8,8,32,128]{3,1,0,2:T(8,128)(2,1)S(1)} %copy.104), channel_id=1, replica_groups=mesh['gx'=4,'gy'=4,'ga'=2] {'gx'}, dimensions={2} | all-to-all | bytes 1048576 | tf_op jit(solution)/shard_map/all_to_all | solution.py:250
  470.4 0.7 fusion.37
  471.1 1.0 copy.106
  (65 shorter events, 7.2 us)
Async XLA Ops:
  6.5 463.9 %copy-start = (bf16[32,32]{1,0:T(8,128)(2,1)S(1)}, bf16[32,32]{1,0:T(8,128)(2,1)}, u32[]{:S(2)}) copy-start(bf16[32,32]{1,0:T(8,128)(2,1)} %param.11) | copy-start | bytes 6148
  6.5 5.3 %copy-start.4 = (f32[5,8,16,256]{3,2,1,0:T(8,128)S(1)}, f32[5,8,16,256]{3,2,1,0:T(8,128)}, u32[]{:S(2)}) copy-start(f32[5,8,16,256]{3,2,1,0:T(8,128)} %param.7) | copy-start | bytes 1966084
  7.8 9.0 %collective-permute-start = (f32[6,8,3,256]{3,1,2,0:T(8,128)S(1)}, f32[6,8,3,256]{3,1,2,0:T(8,128)S(1)}, u32[]{:S(2)}, u32[]{:S(2)}) collective-permute-start(f32[6,8,3,256]{3,1,2,0:T(8,128)S(1)} %copy.159), channel_id=1, source_target_pairs={{0,8},{8,16},{16,24},{24,0},{1,9},{9,17},{17,25},{25,1},{2,10},{10... | collective-permute-start | bytes 442376 | tf_op jit(solution)/shard_map/ppermute | solution.py:23
  10.9 10.0 %collective-permute-start.1 = (f32[6,8,3,256]{3,1,2,0:T(8,128)S(1)}, f32[6,8,3,256]{3,1,2,0:T(8,128)S(1)}, u32[]{:S(2)}, u32[]{:S(2)}) collective-permute-start(f32[6,8,3,256]{3,1,2,0:T(8,128)S(1)} %copy.160), channel_id=1, source_target_pairs={{8,0},{16,8},{24,16},{0,24},{9,1},{17,9},{25,17},{1,25},{10,2},{18... | collective-permute-start | bytes 442376 | tf_op jit(solution)/shard_map/ppermute | solution.py:26
  24.8 8.7 %copy-start.2 = (f32[6,8,3,256]{2,1,3,0:T(8,128)S(1)}, f32[6,8,3,256]{2,1,3,0:T(8,128)}, u32[]{:S(2)}) copy-start(f32[6,8,3,256]{2,1,3,0:T(8,128)} %copy.87) | copy-start | bytes 442372
  26.2 7.0 %collective-permute-start.2 = (f32[6,8,22,3]{2,1,3,0:T(8,128)S(1)}, f32[6,8,22,3]{2,1,3,0:T(8,128)S(1)}, u32[]{:S(2)}, u32[]{:S(2)}) collective-permute-start(f32[6,8,22,3]{2,1,3,0:T(8,128)S(1)} %get-tuple-element.11), channel_id=1, source_target_pairs={{0,2},{2,4},{4,6},{6,0},{1,3},{3,5},{5,7},{7,1},{8,10},{10,12},{12... | collective-permute-start | bytes 38024 | tf_op jit(solution)/shard_map/ppermute | solution.py:23
  28.3 5.2 %collective-permute-start.3 = (f32[6,8,22,3]{2,1,3,0:T(8,128)S(1)}, f32[6,8,22,3]{2,1,3,0:T(8,128)S(1)}, u32[]{:S(2)}, u32[]{:S(2)}) collective-permute-start(f32[6,8,22,3]{2,1,3,0:T(8,128)S(1)} %get-tuple-element.12), channel_id=1, source_target_pairs={{2,0},{4,2},{6,4},{0,6},{3,1},{5,3},{7,5},{1,7},{10,8},{12,10},{14... | collective-permute-start | bytes 38024 | tf_op jit(solution)/shard_map/ppermute | solution.py:26
  40.0 3.7 copy-start.1
  47.8 7.9 %collective-permute-start.4 = (f32[6,3,22,262]{3,2,1,0:T(8,128)}, f32[6,3,22,262]{3,2,1,0:T(8,128)}, u32[]{:S(2)}, u32[]{:S(2)}) collective-permute-start(f32[6,3,22,262]{3,2,1,0:T(8,128)} %copy.88), channel_id=1, source_target_pairs={{0,1},{1,0},{2,3},{3,2},{4,5},{5,4},{6,7},{7,6},{8,9},{9,8},{10,11... | collective-permute-start | bytes 1245032 | tf_op jit(solution)/shard_map/ppermute | solution.py:23
  50.1 5.7 %collective-permute-start.5 = (f32[6,3,22,262]{3,2,1,0:T(8,128)}, f32[6,3,22,262]{3,2,1,0:T(8,128)S(1)}, u32[]{:S(2)}, u32[]{:S(2)}) collective-permute-start(f32[6,3,22,262]{3,2,1,0:T(8,128)} %copy.89), channel_id=1, source_target_pairs={{1,0},{0,1},{3,2},{2,3},{5,4},{4,5},{7,6},{6,7},{9,8},{8,9},{11,10... | collective-permute-start | bytes 1245032 | tf_op jit(solution)/shard_map/ppermute | solution.py:26
  89.5 1.2 copy-start.5
  89.5 1.2 copy-start.6
  93.0 11.9 %all-to-all-start = ((bf16[8,32,8,128]{3,2,0,1:T(8,128)(2,1)}), bf16[8,32,8,128]{3,2,0,1:T(8,128)(2,1)S(1)}, u32[]{:S(2)}, u32[]{:S(2)}) async-start(bf16[8,32,8,128]{3,2,0,1:T(8,128)(2,1)} %copy.94), calls=%async_computation | async-start | bytes 1048576 | tf_op jit(solution)/shard_map/all_to_all | solution.py:194
  105.8 18.2 %all-to-all-start.1 = ((bf16[8,8,32,128]{3,2,1,0:T(8,128)(2,1)}), bf16[8,8,32,128]{3,2,1,0:T(8,128)(2,1)S(1)}, u32[]{:S(2)}, u32[]{:S(2)}) async-start(bf16[8,8,32,128]{3,2,1,0:T(8,128)(2,1)} %bitcast.183), calls=%async_computation.1 | async-start | bytes 1048576 | tf_op jit(solution)/shard_map/all_to_all | solution.py:193
  110.3 60.4 %reduce-scatter.3.cloned.1.call-start = ((), (), s32[]{:S(2)}) async-start(), calls=%async_computation.6 | async-start | bytes 589824 | tf_op jit(solution)/shard_map/reduce_scatter | solution.py:220
  141.1 55.7 %reduce-scatter.5.cloned.1.call-start = ((), (), s32[]{:S(2)}) async-start(), calls=%async_computation.7 | async-start | bytes 786432 | tf_op jit(solution)/shard_map/reduce_scatter | solution.py:231
  181.7 2.2 copy-start.3
  457.7 12.7 %copy-start.7 = (f32[32]{0:T(128)S(1)}, f32[32]{0:T(128)}, u32[]{:S(2)}) copy-start(f32[32]{0:T(128)} %param.13) | copy-start | bytes 388
Sparse Core Ops, SparseCore 0:
  141.2 29.4 reduce-scatter.2
  191.0 5.7 reduce-scatter.4
where the time goes:
time: 483 us; the launch traced here: 479 us
  local copies, waits for them, and re-layouts  239 us (49%)
  blocking collectives  74.9 us (16%)
  waiting for transfers between devices  58.1 us (12%)
  other arithmetic  52.5 us (11%)
  matrix products  22.9 us (5%)
  starting transfers between devices  17.3 us (4%)
  between operations  14.2 us (3%)
    unnamed x32, local copies, waits for them, and re-layouts  136 us
    all_to_all x1, blocking collectives, shards(): lax.all_to_all(back_north, 'gy', split_axis=4, concat_axis=2, tiled=True)  53.4 us
    all_to_all x2, local copies, waits for them, and re-layouts, shards(): lax.all_to_all(back_north, 'gy', split_axis=4, concat_axis=2, tiled=True)  40.6 us
    reduce_scatter x1, waiting for transfers between devices, shards(): lax.psum_scatter(forward_depth_blocks(picked, depth_points, frequencies,...  29.5 us
    dot_general x1, local copies, waits for them, and re-layouts, shards(): jnp.einsum('zomq,qpy->zompy', back_depth, inverse_north_table(north_point...  23.9 us
    all_to_all x1, waiting for transfers between devices, shards(): lax.all_to_all(lax.all_to_all(lifted, 'gx', split_axis=1, concat_axis=2,...  11.9 us
    all_to_all x1, blocking collectives, shards(): lax.all_to_all(spectral, 'gx', split_axis=2, concat_axis=1, tiled=True)  11.4 us
    mul x1, other arithmetic, coarsen(): 0.25 * (blocks[:, :, :, 0, :, 0] + blocks[:, :, :, 1, :, 0] + blocks[:, :...  10.9 us
  transfers between devices with their start and end apart: 10, of which 6 were waited for; matrix products, arithmetic and copies ran while one was open for 4% of the time, Pallas kernels for 0%

commit v1 on v0

--- a/solution.py
+++ b/solution.py
@@ -240,7 +240,10 @@
         inverse_north_table(north_points, length_north, MY),
         precision=highest,
     )
-    all_modes = lax.all_to_all(back_north, "gy", split_axis=4, concat_axis=2, tiled=True)
+    all_modes = jnp.concatenate(
+        lax.all_to_all(jnp.stack(jnp.split(back_north, lax.axis_size("gy"), axis=4)), "gy", 0, 0),
+        axis=2,
+    )
     spectral = jnp.einsum(
         "zompy,mpx->zoxy",
         all_modes,

time: 483 us -> 278 us (0.58)
  local copies, waits for them, and re-layouts: 239 us -> 42.6 us
  other arithmetic: 52.5 us -> 45 us
    unnamed x32 -> x30, local copies, waits for them, and re-layouts: 136 us -> 3.04 us
    all_to_all x2 -> x0, local copies, waits for them, and re-layouts: 40.6 us -> none  [shards(): lax.all_to_all(back_north, 'gy', split_axis=4, concat_axis=2, tiled=True)]
    dot_general x1 -> x0, local copies, waits for them, and re-layouts: 23.9 us -> none  [shards(): jnp.einsum('zomq,qpy->zompy', back_depth, inverse_north_table(north_point...]
    all_to_all x1 -> x0, other arithmetic: 7.72 us -> none  [shards(): lax.all_to_all(back_north, 'gy', split_axis=4, concat_axis=2, tiled=True)]
  transfers between devices with their start and end apart: 10 -> 10, of which waited for: 6 -> 6; matrix products, arithmetic and copies ran while one was open for 4% -> 7% of each run, Pallas kernels for 0% -> 0%
where the time goes in v1:
time: 278 us; the launch traced here: 275 us
  blocking collectives  74.9 us (27%)
  waiting for transfers between devices  57.6 us (21%)
  other arithmetic  45 us (16%)
  local copies, waits for them, and re-layouts  42.6 us (15%)
  matrix products  22.9 us (8%)
  starting transfers between devices  17.8 us (6%)
  between operations  14.1 us (5%)
    all_to_all x1, blocking collectives, shards(): lax.all_to_all(jnp.stack(jnp.split(back_north, lax.axis_size('gy'), axis=...  53.3 us
    reduce_scatter x1, waiting for transfers between devices, shards(): lax.psum_scatter(forward_depth_blocks(picked, depth_points, frequencies,...  29.4 us
    all_to_all x1, waiting for transfers between devices, shards(): lax.all_to_all(lax.all_to_all(lifted, 'gx', split_axis=1, concat_axis=2,...  11.9 us
    all_to_all x1, blocking collectives, shards(): lax.all_to_all(spectral, 'gx', split_axis=2, concat_axis=1, tiled=True)  11.4 us
    mul x1, other arithmetic, coarsen(): 0.25 * (blocks[:, :, :, 0, :, 0] + blocks[:, :, :, 1, :, 0] + blocks[:, :...  10.9 us
    all_gather x1, blocking collectives, shards(): lax.all_gather(coeffs, 'gx', axis=1, tiled=True)  10.2 us
    add x3, other arithmetic, step_interior(): center - courant_half * (transport + coupling) + smooth_half * curvature  8.56 us
    all_to_all x1, waiting for transfers between devices, shards(): lax.all_to_all(lifted, 'gx', split_axis=1, concat_axis=2, tiled=True)  8.4 us
  transfers between devices with their start and end apart: 10, of which 6 were waited for; matrix products, arithmetic and copies ran while one was open for 7% of the time, Pallas kernels for 0%

profile of v1, /device:TPU:0, one launch (start us, length us, event | category | flops | bytes accessed | tf_op | source)
XLA Modules:
  0.0 274.9 jit_solution(11484271271268144863)
XLA Ops:
  6.5 1.2 fusion.68
  7.8 3.0 %collective-permute-start = (f32[6,8,3,256]{3,1,2,0:T(8,128)S(1)}, f32[6,8,3,256]{3,1,2,0:T(8,128)S(1)}, u32[]{:S(2)}, u32[]{:S(2)}) collective-permute-start(f32[6,8,3,256]{3,1,2,0:T(8,128)S(1)} %copy.154), channel_id=1, source_target_pairs={{0,8},{8,16},{16,24},{24,0},{1,9},{9,17},{17,25},{25,1},{2,10},{10... | collective-permute-start | bytes 442376 | tf_op jit(solution)/shard_map/ppermute | solution.py:23
  10.9 1.0 collective-permute-start.1
  11.9 1.0 pad_maximum_fusion.3
  12.9 4.0 %copy.84 = f32[6,8,16,256]{2,1,3,0:T(8,128)} copy(f32[6,8,16,256]{3,2,1,0:T(8,128)S(1)} %pad_maximum_fusion.3) | data formatting | bytes 1572864 | tf_op jit(solution)/shard_map/concatenate | solution.py:174
  16.8 4.0 %copy.83 = f32[6,8,3,256]{2,1,3,0:T(8,128)} copy(f32[6,8,3,256]{3,1,2,0:T(8,128)S(1)} %collective-permute-done) | data formatting | bytes 294912 | tf_op jit(solution)/shard_map/ppermute | solution.py:23
  20.9 4.0 %copy.85 = f32[6,8,3,256]{2,1,3,0:T(8,128)} copy(f32[6,8,3,256]{3,1,2,0:T(8,128)S(1)} %collective-permute-done.1) | data formatting | bytes 294912 | tf_op jit(solution)/shard_map/ppermute | solution.py:26
  24.9 1.4 pad_maximum_fusion.8
  26.3 2.1 collective-permute-start.2
  28.3 2.6 collective-permute-start.3
  30.9 2.1 collective-permute-done.2
  33.0 0.6 collective-permute-done.3
  33.6 6.5 %pad_maximum_fusion = f32[6,8,22,262]{2,1,3,0:T(8,128)S(1)} fusion(f32[6,8,22,3]{2,1,3,0:T(8,128)S(1)} %collective-permute-done.3, f32[6,8,3,256]{2,1,3,0:T(8,128)S(1)} %copy-done.2, f32[6,8,16,256]{2,1,3,0:T(8,128)} %copy.84, f32[6,8,3,256]{2,1,3,0:T(8,128)} %copy.83, f32[6,8,22,3]{2,1,3,0:T(8,128)S(1)} %collective-permute-done.2), kind=kLoop, calls=%fused_computation.1 | loop fusion | flops 1106688 | bytes 2213376 | tf_op jit(solution)/shard_map/concatenate | solution.py:27
  40.1 3.2 %fusion.168 = (f32[6,3,22,262]{2,1,3,0:T(4,128)}, f32[6,3,22,262]{2,1,3,0:T(4,128)S(1)}) fusion(f32[6,8,22,262]{2,1,3,0:T(8,128)S(1)} %pad_maximum_fusion), kind=kLoop, calls=%fused_computation.279 | loop fusion | bytes 1660032 | tf_op jit(solution)/shard_map/slice | solution.py:24
  43.3 0.6 copy-done.1
  43.8 4.0 %copy.86 = f32[6,3,22,262]{3,2,1,0:T(8,128)} copy(f32[6,3,22,262]{2,1,3,0:T(4,128)} %get-tuple-element.13) | data formatting | bytes 830016 | tf_op jit(solution)/shard_map/slice | solution.py:24
  47.9 2.3 copy.87
  50.7 5.1 %copy.88 = f32[6,8,22,262]{3,2,1,0:T(8,128)S(1)} copy(f32[6,8,22,262]{2,1,3,0:T(8,128)} %copy-done.1) | data formatting | bytes 2213376 | tf_op jit(solution)/shard_map/concatenate | solution.py:27
  55.8 1.3 pad_maximum_fusion.1
  57.1 3.0 %slice_subtract_fusion.2 = (f32[5,12,20,260]{3,2,1,0:T(8,128)S(1)}, f32[5,12,20,260]{3,2,1,0:T(8,128)S(1)}, f32[5,12,20,260]{3,2,1,0:T(8,128)S(1)}) fusion(f32[6,14,22,262]{3,2,1,0:T(8,128)S(1)} %pad_maximum_fusion.1), kind=kLoop, calls=%fused_computation.20 | loop fusion | flops 936000 | bytes 11232000 | tf_op jit(solution)/shard_map/sub | solution.py:40
  60.6 4.1 %multiply_add_fusion = f32[5,12,20,260]{3,2,1,0:T(8,128)S(1)} fusion(f32[6,14,22,262]{3,2,1,0:T(8,128)S(1)} %pad_maximum_fusion.1, f32[5,12,20,260]{3,2,1,0:T(8,128)S(1)} %fusion.52, f32[5,12,20,260]{3,2,1,0:T(8,128)S(1)} %get-tuple-element.17, f32[5,12,20,260]{3,2,1,0:T(8,128)S(1)} %get-tuple-element.16, f32[5,12,20,260]{3,2,1,0:T(8,128)S(1)} %get-tuple-element.15), kind=kLoop, calls=%fused_computation.11 | loop fusion | flops 5304000 | bytes 14976000 | tf_op jit(solution)/shard_map/add | solution.py:56
  64.6 2.5 slice_subtract_fusion.5
  67.5 3.3 %multiply_add_fusion.1 = f32[5,10,18,258]{3,2,1,0:T(8,128)S(1)} fusion(f32[5,12,20,260]{3,2,1,0:T(8,128)S(1)} %multiply_add_fusion, f32[5,10,18,258]{3,2,1,0:T(8,128)S(1)} %fusion.60, f32[5,10,18,258]{3,2,1,0:T(8,128)S(1)} %get-tuple-element.19, f32[5,10,18,258]{3,2,1,0:T(8,128)S(1)} %get-tuple-element.20, f32[5,10,18,258]{3,2,1,0:T(8,128)S(1)} %get-tuple-element.18), kind=kLoop, calls=%fused_computation.21 | loop fusion | flops 3947400 | bytes 11145600 | tf_op jit(solution)/shard_map/add | solution.py:56
  70.8 0.9 slice_subtract_fusion.8
  71.9 1.2 multiply_add_fusion.2
  73.1 5.5 %copy.89 = f32[5,8,16,256]{1,3,2,0:T(8,128)} copy(f32[5,8,16,256]{3,2,1,0:T(8,128)S(1)} %multiply_add_fusion.2) | data formatting | bytes 1310720 | tf_op jit(solution)/shard_map/add | solution.py:56
  78.6 10.9 %fusion = f32[5,8,8,1,128,1]{1,5,4,3,2,0:T(1,128)S(1)} fusion(f32[5,8,8,2,128,2]{1,5,4,3,2,0:T(2,128)} %bitcast.188), kind=kLoop, calls=%fused_computation.8 | loop fusion | flops 163840 | bytes 819200 | tf_op jit(solution)/shard_map/mul | solution.py:66
  89.6 1.1 copy.90
  90.7 1.3 fusion.30
  92.1 1.0 copy.92
  93.1 3.5 %all-to-all-start = ((bf16[8,32,8,128]{3,2,0,1:T(8,128)(2,1)}), bf16[8,32,8,128]{3,2,0,1:T(8,128)(2,1)S(1)}, u32[]{:S(2)}, u32[]{:S(2)}) async-start(bf16[8,32,8,128]{3,2,0,1:T(8,128)(2,1)} %copy.92), calls=%async_computation | async-start | bytes 1048576 | tf_op jit(solution)/shard_map/all_to_all | solution.py:194
  96.6 8.4 %all-to-all-done = bf16[8,32,8,128]{3,2,0,1:T(8,128)(2,1)S(1)} async-done(((bf16[8,32,8,128]{3,2,0,1:T(8,128)(2,1)}), bf16[8,32,8,128]{3,2,0,1:T(8,128)(2,1)S(1)}, u32[]{:S(2)}, u32[]{:S(2)}) %all-to-all-start) | async-done | bytes 524320 | tf_op jit(solution)/shard_map/all_to_all | solution.py:194
  105.0 0.9 copy.206
  105.9 4.7 %all-to-all-start.1 = ((bf16[8,8,32,128]{3,2,1,0:T(8,128)(2,1)}), bf16[8,8,32,128]{3,2,1,0:T(8,128)(2,1)S(1)}, u32[]{:S(2)}, u32[]{:S(2)}) async-start(bf16[8,8,32,128]{3,2,1,0:T(8,128)(2,1)} %bitcast.186), calls=%async_computation.1 | async-start | bytes 1048576 | tf_op jit(solution)/shard_map/all_to_all | solution.py:193
  111.0 1.1 fusion.84
  112.5 11.9 %all-to-all-done.1 = bf16[8,8,32,128]{3,2,1,0:T(8,128)(2,1)S(1)} async-done(((bf16[8,8,32,128]{3,2,1,0:T(8,128)(2,1)}), bf16[8,8,32,128]{3,2,1,0:T(8,128)(2,1)S(1)}, u32[]{:S(2)}, u32[]{:S(2)}) %all-to-all-start.1) | async-done | bytes 524320 | tf_op jit(solution)/shard_map/all_to_all | solution.py:193
  125.0 0.5 fusion.48
  125.6 1.8 fusion.20
  127.4 0.6 gather_fusion
  128.0 0.6 fusion.50
  128.6 2.4 fusion.57
  131.0 3.0 %fusion.53 = f32[8,4,8,8,64]{4,1,3,2,0:T(4,128)S(1)} fusion(f32[2,8,8,8,128]{4,0,3,1,2:T(2,128)S(1)} %fusion.50, s32[8,4]{1,0:T(8,128)S(1)} %iota_add_fusion, s32[2]{0:T(128)S(1)} %iota_add_fusion.2), kind=kOutput, calls=%fused_computation.101 | convolution fusion | flops 3146688 | bytes 1048712 | tf_op jit(solution)/shard_map/zcrbn,rkz->rkcbn/dot_general | solution.py:132
  133.9 3.3 %fusion.15 = bf16[8,4,8,8,64]{4,1,3,2,0:T(4,128)(2,1)S(1)} fusion(f32[8,4,8,8,64]{4,1,3,2,0:T(4,128)S(1)} %fusion.57, f32[2,8,8,8,128]{4,0,3,1,2:T(2,128)S(1)} %fusion.50, s32[8,4]{1,0:T(8,128)S(1)} %iota_add_fusion, s32[2]{0:T(128)S(1)} %iota_add_fusion.2), kind=kOutput, calls=%fused_computation.39 | convolution fusion | flops 3408832 | bytes 1310856 | tf_op jit(solution)/shard_map/zcrbn,rkz->rkcbn/dot_general | solution.py:129
  137.2 2.5 fusion.16
  139.8 0.7 pad_maximum_fusion.4
  140.5 0.9 copy.97
  141.5 29.4 %reduce-scatter.3.cloned.1.call-done = bf16[1,4,8,8,128]{4,3,2,1,0:T(8,128)(2,1)} async-done(((bf16[8,4,8,8,128]{4,3,2,1,0:T(8,128)(2,1)}), bf16[1,4,8,8,128]{4,3,2,1,0:T(8,128)(2,1)}) %reduce-scatter.3.cloned.1.call-update) | async-done | bytes 65552 | tf_op jit(solution)/shard_map/reduce_scatter | solution.py:220
  170.9 0.8 copy.98
  171.8 10.2 %all-gather = f32[1,4,32,8,128]{4,3,1,0,2:T(8,128)S(1)} all-gather(f32[1,4,8,8,128]{4,3,1,0,2:T(8,128)S(1)} %copy.98), channel_id=2, replica_groups=mesh['gx'=4,'gy'=4,'ga'=2] {'gx'}, dimensions={2}, use_global_device_ids=true | all-gather | bytes 655360 | tf_op jit(solution)/shard_map/all_gather | solution.py:226
  182.8 1.3 copy-done.3
  184.2 2.4 multiply_reduce_fusion.3
  186.6 0.9 fusion.79
  187.5 0.9 fusion.75
  188.4 0.9 convolution_subtract_fusion.1
  189.3 0.9 convolution_add_fusion.3
  190.1 1.0 pad_maximum_fusion.5
  191.2 0.6 sine_multiply_fusion.1
  191.8 5.1 %reduce-scatter.5.cloned.1.call-done = f32[8,8,8,128]{3,0,2,1:T(8,128)} async-done(((f32[16,8,8,128]{3,0,2,1:T(8,128)}), f32[8,8,8,128]{3,0,2,1:T(8,128)}) %reduce-scatter.5.cloned.1.call-update) | async-done | bytes 262160 | tf_op jit(solution)/shard_map/reduce_scatter | solution.py:231
  196.9 2.7 fusion.41
  200.2 53.3 %all_to_all.50 = f32[4,8,8,8,2,128]{5,3,4,2,1,0:T(8,128)S(1)} all-to-all(f32[4,8,8,8,2,128]{5,3,4,2,1,0:T(8,128)S(1)} %pad_maximum_fusion.2), channel_id=1, replica_groups=mesh['gx'=4,'gy'=4,'ga'=2] {'gy'}, dimensions={0} | all-to-all | bytes 4194304 | tf_op jit(solution)/shard_map/all_to_all | solution.py:244
  253.5 1.1 fusion.17
  254.8 11.4 %all_to_all.51 = bf16[8,8,32,128]{3,1,0,2:T(8,128)(2,1)S(1)} all-to-all(bf16[8,8,32,128]{3,1,0,2:T(8,128)(2,1)S(1)} %copy.101), channel_id=1, replica_groups=mesh['gx'=4,'gy'=4,'ga'=2] {'gx'}, dimensions={2} | all-to-all | bytes 1048576 | tf_op jit(solution)/shard_map/all_to_all | solution.py:253
  266.2 0.7 fusion.38
  266.9 1.0 copy.103
  (61 shorter events, 4.6 us)
Async XLA Ops:
  6.5 259.7 %copy-start = (bf16[32,32]{1,0:T(8,128)(2,1)S(1)}, bf16[32,32]{1,0:T(8,128)(2,1)}, u32[]{:S(2)}) copy-start(bf16[32,32]{1,0:T(8,128)(2,1)} %param.11) | copy-start | bytes 6148
  6.5 5.3 %copy-start.4 = (f32[5,8,16,256]{3,2,1,0:T(8,128)S(1)}, f32[5,8,16,256]{3,2,1,0:T(8,128)}, u32[]{:S(2)}) copy-start(f32[5,8,16,256]{3,2,1,0:T(8,128)} %param.7) | copy-start | bytes 1966084
  7.8 9.0 %collective-permute-start = (f32[6,8,3,256]{3,1,2,0:T(8,128)S(1)}, f32[6,8,3,256]{3,1,2,0:T(8,128)S(1)}, u32[]{:S(2)}, u32[]{:S(2)}) collective-permute-start(f32[6,8,3,256]{3,1,2,0:T(8,128)S(1)} %copy.154), channel_id=1, source_target_pairs={{0,8},{8,16},{16,24},{24,0},{1,9},{9,17},{17,25},{25,1},{2,10},{10... | collective-permute-start | bytes 442376 | tf_op jit(solution)/shard_map/ppermute | solution.py:23
  10.9 10.0 %collective-permute-start.1 = (f32[6,8,3,256]{3,1,2,0:T(8,128)S(1)}, f32[6,8,3,256]{3,1,2,0:T(8,128)S(1)}, u32[]{:S(2)}, u32[]{:S(2)}) collective-permute-start(f32[6,8,3,256]{3,1,2,0:T(8,128)S(1)} %copy.155), channel_id=1, source_target_pairs={{8,0},{16,8},{24,16},{0,24},{9,1},{17,9},{25,17},{1,25},{10,2},{18... | collective-permute-start | bytes 442376 | tf_op jit(solution)/shard_map/ppermute | solution.py:26
  24.9 8.7 %copy-start.2 = (f32[6,8,3,256]{2,1,3,0:T(8,128)S(1)}, f32[6,8,3,256]{2,1,3,0:T(8,128)}, u32[]{:S(2)}) copy-start(f32[6,8,3,256]{2,1,3,0:T(8,128)} %copy.85) | copy-start | bytes 442372
  26.3 6.8 %collective-permute-start.2 = (f32[6,8,22,3]{2,1,3,0:T(8,128)S(1)}, f32[6,8,22,3]{2,1,3,0:T(8,128)S(1)}, u32[]{:S(2)}, u32[]{:S(2)}) collective-permute-start(f32[6,8,22,3]{2,1,3,0:T(8,128)S(1)} %get-tuple-element.11), channel_id=1, source_target_pairs={{0,2},{2,4},{4,6},{6,0},{1,3},{3,5},{5,7},{7,1},{8,10},{10,12},{12... | collective-permute-start | bytes 38024 | tf_op jit(solution)/shard_map/ppermute | solution.py:23
  28.3 5.2 %collective-permute-start.3 = (f32[6,8,22,3]{2,1,3,0:T(8,128)S(1)}, f32[6,8,22,3]{2,1,3,0:T(8,128)S(1)}, u32[]{:S(2)}, u32[]{:S(2)}) collective-permute-start(f32[6,8,22,3]{2,1,3,0:T(8,128)S(1)} %get-tuple-element.12), channel_id=1, source_target_pairs={{2,0},{4,2},{6,4},{0,6},{3,1},{5,3},{7,5},{1,7},{10,8},{12,10},{14... | collective-permute-start | bytes 38024 | tf_op jit(solution)/shard_map/ppermute | solution.py:26
  40.1 3.7 %copy-start.1 = (f32[6,8,22,262]{2,1,3,0:T(8,128)}, f32[6,8,22,262]{2,1,3,0:T(8,128)S(1)}, u32[]{:S(2)}) copy-start(f32[6,8,22,262]{2,1,3,0:T(8,128)S(1)} %pad_maximum_fusion) | copy-start | bytes 3320068
  47.9 7.9 %collective-permute-start.4 = (f32[6,3,22,262]{3,2,1,0:T(8,128)}, f32[6,3,22,262]{3,2,1,0:T(8,128)}, u32[]{:S(2)}, u32[]{:S(2)}) collective-permute-start(f32[6,3,22,262]{3,2,1,0:T(8,128)} %copy.86), channel_id=1, source_target_pairs={{0,1},{1,0},{2,3},{3,2},{4,5},{5,4},{6,7},{7,6},{8,9},{9,8},{10,11... | collective-permute-start | bytes 1245032 | tf_op jit(solution)/shard_map/ppermute | solution.py:23
  50.2 5.7 %collective-permute-start.5 = (f32[6,3,22,262]{3,2,1,0:T(8,128)}, f32[6,3,22,262]{3,2,1,0:T(8,128)S(1)}, u32[]{:S(2)}, u32[]{:S(2)}) collective-permute-start(f32[6,3,22,262]{3,2,1,0:T(8,128)} %copy.87), channel_id=1, source_target_pairs={{1,0},{0,1},{3,2},{2,3},{5,4},{4,5},{7,6},{6,7},{9,8},{8,9},{11,10... | collective-permute-start | bytes 1245032 | tf_op jit(solution)/shard_map/ppermute | solution.py:26
  89.5 1.2 copy-start.5
  89.5 1.2 copy-start.6
  93.1 11.9 %all-to-all-start = ((bf16[8,32,8,128]{3,2,0,1:T(8,128)(2,1)}), bf16[8,32,8,128]{3,2,0,1:T(8,128)(2,1)S(1)}, u32[]{:S(2)}, u32[]{:S(2)}) async-start(bf16[8,32,8,128]{3,2,0,1:T(8,128)(2,1)} %copy.92), calls=%async_computation | async-start | bytes 1048576 | tf_op jit(solution)/shard_map/all_to_all | solution.py:194
  105.9 18.5 %all-to-all-start.1 = ((bf16[8,8,32,128]{3,2,1,0:T(8,128)(2,1)}), bf16[8,8,32,128]{3,2,1,0:T(8,128)(2,1)S(1)}, u32[]{:S(2)}, u32[]{:S(2)}) async-start(bf16[8,8,32,128]{3,2,1,0:T(8,128)(2,1)} %bitcast.186), calls=%async_computation.1 | async-start | bytes 1048576 | tf_op jit(solution)/shard_map/all_to_all | solution.py:193
  110.6 60.3 %reduce-scatter.3.cloned.1.call-start = ((), (), s32[]{:S(2)}) async-start(), calls=%async_computation.6 | async-start | bytes 589824 | tf_op jit(solution)/shard_map/reduce_scatter | solution.py:220
  141.4 55.5 %reduce-scatter.5.cloned.1.call-start = ((), (), s32[]{:S(2)}) async-start(), calls=%async_computation.7 | async-start | bytes 786432 | tf_op jit(solution)/shard_map/reduce_scatter | solution.py:231
  182.0 2.2 copy-start.3
  253.5 12.7 %copy-start.7 = (f32[32]{0:T(128)S(1)}, f32[32]{0:T(128)}, u32[]{:S(2)}) copy-start(f32[32]{0:T(128)} %param.13) | copy-start | bytes 388
Sparse Core Ops, SparseCore 0:
  141.6 29.2 reduce-scatter.2
  191.3 5.5 reduce-scatter.4
